TPU v7x, 32 devices: a whole 2x2x4 slice. The times are simulated.
32 devices in a mesh: groups: 2 (over y), text: 4 (over z), image: 4 (over x, core).
Axes of the slice: x: 2, y: 2, z: 4, core: 2. Of those that a mesh axis runs over, the one named last changes fastest.
Arguments:
- text_states: bfloat16 [1024, 8192], P(('groups', 'text')), parts along dimension 0, may hold values from -6 to 6
- grid_levels: bfloat16 [16384, 8192], P(('groups', 'text'), 'image'), parts along dimension 0, may hold values from -8 to 7, as said below
- round_logits: float32 [16384, 8192], P(('groups', 'text'), 'image'), parts along dimension 0, may hold values from -2 to 2
- column_steps: float32 [16384], P(('groups', 'image')), parts along dimension 0, may hold values from 0.0015 to 0.004
- image_keys: bfloat16 [12808, 1024], P('groups', 'image'), parts along dimension 0, may hold values from -500 to 500
- image_values: bfloat16 [12808, 1024], P('groups', 'image'), parts along dimension 0, may hold values from -6 to 6
- target_out: bfloat16 [1024, 8192], P(('groups', 'text'), 'image'), parts along dimension 0, may hold values from -6 to 6
- doc_images: int32 [6], P('groups'), parts along dimension 0, may hold values from 1 to 2, as said below
- image_start: int32 [8], P('groups'), parts along dimension 0, may hold values from 1 to 3, as said below
Outputs:
- rounding_grad: float32 [16384, 8192], P(('groups', 'text'), 'image'), parts along dimension 0
There are 2 independent parts, one for each index of `groups`. A program takes and returns all parts, laid end to end along the dimension named above; each array names one. Nothing has to cross between parts.
Inputs may be any that keep to these rules, and one draw needn't show every extreme that they name: `doc_images`: every document holds one image or more, 4 in all; one document holds exactly 2, and no document more. `image_start`: Nondecreasing; the first image's entry is 1 and the last image's 4 - 1. `grid_levels`: whole numbers.
All inputs are finite; a program needn't handle non-finite values.
Results may differ from a plain program's by a relative error of at most 0.015.
Values may be sent and summed in bfloat16 or wider, within the bound.
A program may use at most 256 MiB of HBM per device.

v0:
```python
import jax
import jax.numpy as jnp
from jax import lax
from jax.sharding import PartitionSpec as P

H = 64
KVH = 8
HD = 128
IMAGES = 4
IMG_TOK = 1601
SPAN = 128


def visibility(span_ids, doc_images, image_start, total_spans):
    images = image_start.shape[0]
    documents = doc_images.shape[0]
    doc_ends = jnp.cumsum(doc_images)
    positions = jnp.arange(images, dtype=jnp.int32)
    doc_of = jnp.sum((positions[:, None] >= doc_ends[None, :]).astype(jnp.int32), axis=1)
    doc_index = jnp.arange(documents, dtype=jnp.int32)
    end_of = jnp.sum(jnp.where(doc_index[None, :] == doc_of[:, None], doc_ends[None, :], 0), axis=1)
    stop_at = jnp.sum(
        jnp.where(positions[None, :] == end_of[:, None], image_start[None, :], 0), axis=1
    )
    stop_at = stop_at + jnp.where(end_of >= images, total_spans, 0)
    return (span_ids[:, None] >= image_start[None, :]) & (span_ids[:, None] < stop_at[None, :])


def head_grad(queries, keys, values, target, visible):
    tokens_here = queries.shape[0]
    kv_heads = queries.shape[1]
    per_group = queries.shape[2]
    head_size = queries.shape[3]
    scaling = head_size ** (-0.5)
    shape = (kv_heads, per_group, tokens_here)

    def tile_of(which):
        keys_now = lax.dynamic_slice_in_dim(keys, which * IMG_TOK, IMG_TOK, 0)
        values_now = lax.dynamic_slice_in_dim(values, which * IMG_TOK, IMG_TOK, 0)
        scores = (
            jnp.einsum("tkgd,nkd->kgtn", queries, keys_now, preferred_element_type=jnp.float32)
            * scaling
        )
        return (scores, keys_now, values_now)

    def seen_of(which):
        return lax.dynamic_index_in_dim(visible, which, 1, keepdims=False)

    def forward(which, state):
        seen_rows = seen_of(which)
        running, total, accum = state
        scores, keys_now, values_now = tile_of(which)
        seen = seen_rows[None, None, :]
        peak = jnp.where(seen, jnp.maximum(running, jnp.max(scores, axis=-1)), running)
        weights = jnp.where(seen[..., None], jnp.exp(scores - peak[..., None]), 0.0)
        fade = jnp.exp(running - peak)
        total = total * fade + jnp.sum(weights, axis=-1)
        product = jnp.einsum(
            "kgtn,nkd->kgtd",
            weights.astype(jnp.bfloat16),
            values_now,
            preferred_element_type=jnp.float32,
        )
        return (peak, total, accum * fade[..., None] + product)

    start_state = (
        jnp.full(shape, -1e30, jnp.float32),
        jnp.zeros(shape, jnp.float32),
        jnp.zeros(shape + (head_size,), jnp.float32),
    )
    running, total, accum = lax.fori_loop(0, IMAGES, forward, start_state)
    denom = jnp.maximum(total, 1.0)
    attended = accum / denom[..., None]
    out_grad = (1024.0 * (attended - target)).astype(jnp.bfloat16)
    delta = jnp.sum(out_grad.astype(jnp.float32) * attended, axis=-1)

    def backward(which, grad_acc):
        seen_rows = seen_of(which)
        scores, keys_now, values_now = tile_of(which)
        seen = seen_rows[None, None, :]
        probs = (
            jnp.where(seen[..., None], jnp.exp(scores - running[..., None]), 0.0) / denom[..., None]
        )
        dprob = jnp.einsum(
            "kgtd,nkd->kgtn", out_grad, values_now, preferred_element_type=jnp.float32
        )
        score_grad = (probs * (dprob - delta[..., None]) * scaling).astype(jnp.bfloat16)
        return grad_acc + jnp.einsum(
            "kgtn,nkd->kgtd", score_grad, keys_now, preferred_element_type=jnp.float32
        )

    grad_sum = lax.fori_loop(0, IMAGES, backward, jnp.zeros(shape + (head_size,), jnp.float32))
    return grad_sum.astype(jnp.bfloat16)


def per_device(
    text_states,
    grid_levels,
    round_logits,
    column_steps,
    image_keys,
    image_values,
    target_out,
    doc_images,
    image_start,
):
    tok_dev = text_states.shape[0]
    out_cols = grid_levels.shape[1]
    n_text = lax.axis_size("text")
    per_group = H // KVH
    kvh_dev = image_keys.shape[1] // HD
    sigmoid_v = jax.nn.sigmoid(round_logits)
    soft = 1.2 * sigmoid_v - 0.1
    weight_q = (column_steps[None, :] * (grid_levels.astype(jnp.float32) + soft)).astype(
        jnp.bfloat16
    )
    spread = lax.all_to_all(text_states, "text", split_axis=1, concat_axis=0, tiled=True)
    q_part = jnp.dot(spread, weight_q, preferred_element_type=jnp.float32)
    q_sum = lax.psum_scatter(q_part, "text", scatter_dimension=0, tiled=True)
    queries = q_sum.astype(jnp.bfloat16)
    first_token = lax.axis_index("text") * tok_dev
    span_ids = (first_token + jnp.arange(tok_dev, dtype=jnp.int32)) // SPAN
    visible = visibility(span_ids, doc_images, image_start, n_text * tok_dev // SPAN)
    query_tiles = queries.reshape(tok_dev, kvh_dev, per_group, HD)
    key_tiles = image_keys.reshape(image_keys.shape[0], kvh_dev, HD)
    value_tiles = image_values.reshape(image_values.shape[0], kvh_dev, HD)
    target_tiles = (
        target_out.astype(jnp.float32)
        .reshape(tok_dev, kvh_dev, per_group, HD)
        .transpose(1, 2, 0, 3)
    )
    grads = head_grad(query_tiles, key_tiles, value_tiles, target_tiles, visible)
    query_grad = grads.transpose(2, 0, 1, 3).reshape(tok_dev, out_cols)
    weight_grad = lax.dot_general(
        spread,
        lax.all_gather(query_grad, "text", axis=0, tiled=True),
        (((0,), (0,)), ((), ())),
        preferred_element_type=jnp.float32,
    )
    hprime = 1.2 * sigmoid_v * (1.0 - sigmoid_v)
    centered = 2.0 * soft - 1.0
    return (weight_grad * column_steps[None, :] - 4.0 * centered * centered * centered) * hprime


def solution(mesh):
    placed = (
        P(("groups", "text"), None),
        P(("groups", "text"), "image"),
        P(("groups", "text"), "image"),
        P(("groups", "image")),
        P("groups", "image"),
        P("groups", "image"),
        P(("groups", "text"), "image"),
        P("groups"),
        P("groups"),
    )
    return jax.shard_map(
        per_device,
        mesh=mesh,
        in_specs=placed,
        out_specs=P(("groups", "text"), "image"),
        check_vma=False,
    )
```

profile of v0, /device:TPU:0, one launch (start us, length us, event | category | flops | bytes accessed | tf_op | source)
XLA Modules:
  0.0 431.3 jit_solution(5376205303469265212)
XLA Ops:
  16.9 17.6 %copy.62 = f32[2048,2048]{0,1:T(8,128)} copy(f32[2048,2048]{1,0:T(8,128)} %param.15) | data formatting | bytes 33554432 | tf_op args[2]
  34.5 12.3 %copy.61 = bf16[2048,2048]{0,1:T(8,128)(2,1)} copy(bf16[2048,2048]{1,0:T(8,128)(2,1)} %param.14) | data formatting | bytes 16777216 | tf_op args[1]
  46.8 18.3 %all-to-all-done = bf16[128,4,2048]{0,2,1:T(8,128)(2,1)S(1)} async-done(((bf16[128,4,2048]{0,2,1:T(8,128)(2,1)}), bf16[128,4,2048]{0,2,1:T(8,128)(2,1)S(1)}, u32[]{:S(2)}, u32[]{:S(2)}) %all-to-all-start) | async-done | bytes 2097184 | tf_op jit(solution)/shard_map/all_to_all | solution.py:117
  67.8 14.2 %fusion.47 = f32[512,2048]{0,1:T(8,128)} fusion(bf16[512,2048]{1,0:T(8,128)(2,1)} %bitcast.138, bf16[2048,2048]{0,1:T(8,128)(2,1)} %copy.61, f32[2048]{0:T(1024)S(1)} %copy-done.4, f32[2048,2048]{0,1:T(8,128)} %copy.62), kind=kOutput, calls=%fused_computation.54 | convolution fusion | flops 4332716032 | bytes 31465472 | tf_op jit(solution)/shard_map/dot_general | solution.py:118
  100.3 57.7 %reduce-scatter.2.cloned.1.call-done = f32[128,2048]{0,1:T(8,128)} async-done(((f32[512,2048]{0,1:T(8,128)}), f32[128,2048]{0,1:T(8,128)}) %reduce-scatter.2.cloned.1.call-update) | async-done | bytes 1048592 | tf_op jit(solution)/shard_map/reduce_scatter | solution.py:119
  159.6 94.7 %while.32 = (s32[]{:T(128)}, f32[2,8,128]{2,1,0:T(8,128)S(1)}, f32[2,8,128]{2,1,0:T(8,128)S(1)}, f32[2,8,128,128]{3,2,1,0:T(8,128)}, pred[128,4]{0,1:T(4,128)(4,...) while((s32[]{:T(128)}, f32[2,8,128]{2,1,0:T(8,128)S(1)}, ...), condition=%wide.region_8.9_spmd.clone, body=%wide.region_5.8_spmd.clone.sunk | while | flops 1712357376 | bytes 52192112 | solution.py:71
  159.6 7.8 %bitcast_reduce_fusion.2 = (f32[2,8,128]{2,1,0:T(8,128)S(1)}, f32[2,1601,128,8]{2,1,3,0:T(8,128)}) fusion(bf16[128,2,8,128]{3,0,2,1:T(8,128)(2,1)S(1)} %get-tuple-element.659, bf16[6404,2,128]{2,0,1:T(8,128)(2,1)} %get-tuple-element.658, s32[]{:T(128)S(6)} %select_n.117), kind=kOutput, calls=%fused_computation.1.clone.1 | convolution fusion | flops 845940736 | bytes 14471172 | tf_op jit(solution)/shard_map/while/body/eval_jaxpr/tkgd,nkd->kgtn/dot_general | solution.py:41
  174.8 7.5 %fusion.79 = f32[2,8,128,128]{3,2,1,0:T(8,128)S(1)} fusion(f32[2,1601,128,8]{2,1,3,0:T(8,128)} %get-tuple-element.616, f32[2,8,128]{2,1,0:T(8,128)S(1)} %maximum_select_fusion.2, pred[128]{0:T(512)(128)(4,1)S(1)} %dynamic-slice_bitcast_fusion.4, f32[2,8,128,128]{3,2,1,0:T(8,128)S(1)} %copy-done.1, bf16[6404,2,128]{2,0,1:T(8,128)(2,1)} %get-tuple-element.660, ...), kind=kOutput, calls=%fused_computation.8.clone.1 | convolution fusion | flops 853286912 | bytes 16109701 | tf_op jit(solution)/shard_map/while/body/eval_jaxpr/kgtn,nkd->kgtd/dot_general | solution.py:58
  183.3 7.8 %bitcast_reduce_fusion.2 = (f32[2,8,128]{2,1,0:T(8,128)S(1)}, f32[2,1601,128,8]{2,1,3,0:T(8,128)}) fusion(bf16[128,2,8,128]{3,0,2,1:T(8,128)(2,1)S(1)} %get-tuple-element.659, bf16[6404,2,128]{2,0,1:T(8,128)(2,1)} %get-tuple-element.658, s32[]{:T(128)S(6)} %select_n.117), kind=kOutput, calls=%fused_computation.1.clone.1 | convolution fusion | flops 845940736 | bytes 14471172 | tf_op jit(solution)/shard_map/while/body/eval_jaxpr/tkgd,nkd->kgtn/dot_general | solution.py:41
  206.9 7.8 %bitcast_reduce_fusion.2 = (f32[2,8,128]{2,1,0:T(8,128)S(1)}, f32[2,1601,128,8]{2,1,3,0:T(8,128)}) fusion(bf16[128,2,8,128]{3,0,2,1:T(8,128)(2,1)S(1)} %get-tuple-element.659, bf16[6404,2,128]{2,0,1:T(8,128)(2,1)} %get-tuple-element.658, s32[]{:T(128)S(6)} %select_n.117), kind=kOutput, calls=%fused_computation.1.clone.1 | convolution fusion | flops 845940736 | bytes 14471172 | tf_op jit(solution)/shard_map/while/body/eval_jaxpr/tkgd,nkd->kgtn/dot_general | solution.py:41
  222.1 7.5 %fusion.79 = f32[2,8,128,128]{3,2,1,0:T(8,128)S(1)} fusion(f32[2,1601,128,8]{2,1,3,0:T(8,128)} %get-tuple-element.616, f32[2,8,128]{2,1,0:T(8,128)S(1)} %maximum_select_fusion.2, pred[128]{0:T(512)(128)(4,1)S(1)} %dynamic-slice_bitcast_fusion.4, f32[2,8,128,128]{3,2,1,0:T(8,128)S(1)} %copy-done.1, bf16[6404,2,128]{2,0,1:T(8,128)(2,1)} %get-tuple-element.660, ...), kind=kOutput, calls=%fused_computation.8.clone.1 | convolution fusion | flops 853286912 | bytes 16109701 | tf_op jit(solution)/shard_map/while/body/eval_jaxpr/kgtn,nkd->kgtd/dot_general | solution.py:58
  230.6 7.8 %bitcast_reduce_fusion.2 = (f32[2,8,128]{2,1,0:T(8,128)S(1)}, f32[2,1601,128,8]{2,1,3,0:T(8,128)}) fusion(bf16[128,2,8,128]{3,0,2,1:T(8,128)(2,1)S(1)} %get-tuple-element.659, bf16[6404,2,128]{2,0,1:T(8,128)(2,1)} %get-tuple-element.658, s32[]{:T(128)S(6)} %select_n.117), kind=kOutput, calls=%fused_computation.1.clone.1 | convolution fusion | flops 845940736 | bytes 14471172 | tf_op jit(solution)/shard_map/while/body/eval_jaxpr/tkgd,nkd->kgtn/dot_general | solution.py:41
  256.5 83.1 %while.33 = (s32[]{:T(128)}, f32[2,8,128,128]{3,2,1,0:T(8,128)}, pred[128,4]{0,1:T(4,128)(4,1)S(1)}, bf16[6404,2,128]{2,0,1:T(8,128)(2,1)}, bf16[128,2,8,128]{3,...) while((s32[]{:T(128)}, f32[2,8,128,128]{3,2,1,0:T(8,128)}, ...), condition=%wide.region_11.12_spmd.clone, body=%wide.region_10.11_spmd.clone.sunk | while | flops 2544910336 | bytes 31930436 | solution.py:92
  256.7 7.9 %fusion.85 = f32[2,1601,128,8]{2,1,3,0:T(8,128)} fusion(bf16[128,2,8,128]{3,0,2,1:T(8,128)(2,1)S(1)} %get-tuple-element.697, bf16[6404,2,128]{2,0,1:T(8,128)(2,1)} %get-tuple-element.696, s32[]{:T(128)S(6)} %select_n.119), kind=kOutput, calls=%fused_computation.35.clone.1 | convolution fusion | flops 839385088 | bytes 14462980 | tf_op jit(solution)/shard_map/while/body/eval_jaxpr/tkgd,nkd->kgtn/dot_general | solution.py:41
  264.6 12.7 %fusion.86 = f32[2,8,128,128]{3,2,1,0:T(8,128)} fusion(f32[2,1601,128,8]{2,1,3,0:T(8,128)} %fusion.85, bf16[2,8,128,128]{3,2,1,0:T(8,128)(2,1)S(1)} %get-tuple-element.701, f32[2,8,128]{2,1,0:T(8,128)S(1)} %get-tuple-element.702, f32[2,8,128]{2,1,0:T(8,128)S(1)} %get-tuple-element.699, f32[2,8,128]{2,1,0:T(8,128)S(1)} %get-tuple-element.698, ...), kind=kOutput, calls=%fused_computation.32.clone.1 | convolution fusion | flops 1705525248 | bytes 17467008 | tf_op jit(solution)/shard_map/while/body/eval_jaxpr/kgtn,nkd->kgtd/dot_general | solution.py:88
  277.3 7.7 %fusion.85 = f32[2,1601,128,8]{2,1,3,0:T(8,128)} fusion(bf16[128,2,8,128]{3,0,2,1:T(8,128)(2,1)S(1)} %get-tuple-element.697, bf16[6404,2,128]{2,0,1:T(8,128)(2,1)} %get-tuple-element.696, s32[]{:T(128)S(6)} %select_n.119), kind=kOutput, calls=%fused_computation.35.clone.1 | convolution fusion | flops 839385088 | bytes 14462980 | tf_op jit(solution)/shard_map/while/body/eval_jaxpr/tkgd,nkd->kgtn/dot_general | solution.py:41
  285.1 13.0 %fusion.86 = f32[2,8,128,128]{3,2,1,0:T(8,128)} fusion(f32[2,1601,128,8]{2,1,3,0:T(8,128)} %fusion.85, bf16[2,8,128,128]{3,2,1,0:T(8,128)(2,1)S(1)} %get-tuple-element.701, f32[2,8,128]{2,1,0:T(8,128)S(1)} %get-tuple-element.702, f32[2,8,128]{2,1,0:T(8,128)S(1)} %get-tuple-element.699, f32[2,8,128]{2,1,0:T(8,128)S(1)} %get-tuple-element.698, ...), kind=kOutput, calls=%fused_computation.32.clone.1 | convolution fusion | flops 1705525248 | bytes 17467008 | tf_op jit(solution)/shard_map/while/body/eval_jaxpr/kgtn,nkd->kgtd/dot_general | solution.py:88
  298.1 7.7 %fusion.85 = f32[2,1601,128,8]{2,1,3,0:T(8,128)} fusion(bf16[128,2,8,128]{3,0,2,1:T(8,128)(2,1)S(1)} %get-tuple-element.697, bf16[6404,2,128]{2,0,1:T(8,128)(2,1)} %get-tuple-element.696, s32[]{:T(128)S(6)} %select_n.119), kind=kOutput, calls=%fused_computation.35.clone.1 | convolution fusion | flops 839385088 | bytes 14462980 | tf_op jit(solution)/shard_map/while/body/eval_jaxpr/tkgd,nkd->kgtn/dot_general | solution.py:41
  305.8 13.0 %fusion.86 = f32[2,8,128,128]{3,2,1,0:T(8,128)} fusion(f32[2,1601,128,8]{2,1,3,0:T(8,128)} %fusion.85, bf16[2,8,128,128]{3,2,1,0:T(8,128)(2,1)S(1)} %get-tuple-element.701, f32[2,8,128]{2,1,0:T(8,128)S(1)} %get-tuple-element.702, f32[2,8,128]{2,1,0:T(8,128)S(1)} %get-tuple-element.699, f32[2,8,128]{2,1,0:T(8,128)S(1)} %get-tuple-element.698, ...), kind=kOutput, calls=%fused_computation.32.clone.1 | convolution fusion | flops 1705525248 | bytes 17467008 | tf_op jit(solution)/shard_map/while/body/eval_jaxpr/kgtn,nkd->kgtd/dot_general | solution.py:88
  318.8 7.7 %fusion.85 = f32[2,1601,128,8]{2,1,3,0:T(8,128)} fusion(bf16[128,2,8,128]{3,0,2,1:T(8,128)(2,1)S(1)} %get-tuple-element.697, bf16[6404,2,128]{2,0,1:T(8,128)(2,1)} %get-tuple-element.696, s32[]{:T(128)S(6)} %select_n.119), kind=kOutput, calls=%fused_computation.35.clone.1 | convolution fusion | flops 839385088 | bytes 14462980 | tf_op jit(solution)/shard_map/while/body/eval_jaxpr/tkgd,nkd->kgtn/dot_general | solution.py:41
  326.6 13.0 %fusion.86 = f32[2,8,128,128]{3,2,1,0:T(8,128)} fusion(f32[2,1601,128,8]{2,1,3,0:T(8,128)} %fusion.85, bf16[2,8,128,128]{3,2,1,0:T(8,128)(2,1)S(1)} %get-tuple-element.701, f32[2,8,128]{2,1,0:T(8,128)S(1)} %get-tuple-element.702, f32[2,8,128]{2,1,0:T(8,128)S(1)} %get-tuple-element.699, f32[2,8,128]{2,1,0:T(8,128)S(1)} %get-tuple-element.698, ...), kind=kOutput, calls=%fused_computation.32.clone.1 | convolution fusion | flops 1705525248 | bytes 17467008 | tf_op jit(solution)/shard_map/while/body/eval_jaxpr/kgtn,nkd->kgtd/dot_general | solution.py:88
  341.8 46.9 %all-gather.2.cloned.1.call-done = bf16[512,2048]{0,1:T(8,128)(2,1)} async-done(((bf16[128,2048]{0,1:T(8,128)(2,1)}), bf16[512,2048]{0,1:T(8,128)(2,1)}) %all-gather.2.cloned.1.call-update) | async-done | bytes 2097168 | tf_op jit(solution)/shard_map/all_gather | solution.py:136
  388.7 18.2 %fusion.42 = f32[2048,2048]{0,1:T(8,128)} fusion(bf16[512,2048]{0,1:T(8,128)(2,1)} %all-gather.2.cloned.1.call-done, bf16[512,2048]{1,0:T(8,128)(2,1)S(1)} %bitcast.139, f32[2048]{0:T(1024)S(1)} %copy-done.5, f32[2048,2048]{0,1:T(8,128)} %copy.62), kind=kOutput, calls=%fused_computation.47 | convolution fusion | flops 4357881856 | bytes 37756928 | tf_op jit(solution)/shard_map/dot_general | solution.py:134
  406.9 17.6 %copy.76 = f32[2048,2048]{1,0:T(8,128)} copy(f32[2048,2048]{0,1:T(8,128)} %fusion.42) | data formatting | bytes 33554432 | tf_op jit(solution)/shard_map/mul | solution.py:142
  (82 shorter events, 85.5 us)
Async XLA Ops:
  10.6 54.5 %all-to-all-start = ((bf16[128,4,2048]{0,2,1:T(8,128)(2,1)}), bf16[128,4,2048]{0,2,1:T(8,128)(2,1)S(1)}, u32[]{:S(2)}, u32[]{:S(2)}) async-start(bf16[128,4,2048]{0,2,1:T(8,128)(2,1)} %bitcast.134), calls=%async_computation | async-start | bytes 4194304 | tf_op jit(solution)/shard_map/all_to_all | solution.py:117
  16.9 141.1 %reduce-scatter.2.cloned.1.call-start = ((), (), s32[]{:S(2)}) async-start(), calls=%async_computation.2 | async-start | bytes 5242880 | tf_op jit(solution)/shard_map/reduce_scatter | solution.py:119
  34.5 33.3 %copy-start.4 = (f32[2048]{0:T(1024)S(1)}, f32[2048]{0:T(1024)}, u32[]{:S(2)}) copy-start(f32[2048]{0:T(1024)} %param.16) | copy-start | bytes 24580
  67.8 14.5 %copy-start.6 = (s32[3]{0:T(128)S(1)}, s32[3]{0:T(128)}, u32[]{:S(2)}) copy-start(s32[3]{0:T(128)} %param.20) | copy-start | bytes 40
  82.0 306.7 %all-gather.2.cloned.1.call-start = ((), (), s32[]{:S(2)}) async-start(), calls=%async_computation.3 | async-start | bytes 2621440 | tf_op jit(solution)/shard_map/all_gather | solution.py:136
  82.5 17.5 %copy-start.3 = (s32[4]{0:T(128)S(1)}, s32[4]{0:T(128)}, u32[]{:S(2)}) copy-start(s32[4]{0:T(128)} %param.21) | copy-start | bytes 52
  159.6 15.2 %copy-start.1 = (f32[2,8,128,128]{3,2,1,0:T(8,128)S(1)}, f32[2,8,128,128]{3,2,1,0:T(8,128)}, u32[]{:S(2)}) copy-start(f32[2,8,128,128]{3,2,1,0:T(8,128)} %get-tuple-element.644) | copy-start | bytes 3145732 | tf_op jit(solution)/shard_map/while
  182.3 1.0 copy-start.2
  183.3 15.2 %copy-start.1 = (f32[2,8,128,128]{3,2,1,0:T(8,128)S(1)}, f32[2,8,128,128]{3,2,1,0:T(8,128)}, u32[]{:S(2)}) copy-start(f32[2,8,128,128]{3,2,1,0:T(8,128)} %get-tuple-element.644) | copy-start | bytes 3145732 | tf_op jit(solution)/shard_map/while
  205.9 1.0 copy-start.2
  206.9 15.2 %copy-start.1 = (f32[2,8,128,128]{3,2,1,0:T(8,128)S(1)}, f32[2,8,128,128]{3,2,1,0:T(8,128)}, u32[]{:S(2)}) copy-start(f32[2,8,128,128]{3,2,1,0:T(8,128)} %get-tuple-element.644) | copy-start | bytes 3145732 | tf_op jit(solution)/shard_map/while
  229.6 1.0 copy-start.2
  230.6 15.2 %copy-start.1 = (f32[2,8,128,128]{3,2,1,0:T(8,128)S(1)}, f32[2,8,128,128]{3,2,1,0:T(8,128)}, u32[]{:S(2)}) copy-start(f32[2,8,128,128]{3,2,1,0:T(8,128)} %get-tuple-element.644) | copy-start | bytes 3145732 | tf_op jit(solution)/shard_map/while
  253.3 1.0 copy-start.2
  256.5 132.2 %copy-start = (bf16[4,128,2048]{2,1,0:T(8,128)(2,1)S(1)}, bf16[4,128,2048]{2,1,0:T(8,128)(2,1)}, u32[]{:S(2)}) copy-start(bf16[4,128,2048]{2,1,0:T(8,128)(2,1)} %copy.64) | copy-start | bytes 6291460
  256.5 132.2 %copy-start.5 = (f32[2048]{0:T(1024)S(1)}, f32[2048]{0:T(1024)}, u32[]{:S(2)}) copy-start(f32[2048]{0:T(1024)} %param.16) | copy-start | bytes 24580
Sparse Core Ops, SparseCore 0:
  82.2 75.8 reduce-scatter.1
  341.9 46.7 all-gather.1
where the time goes:
time: 433 us; the launch traced here: 431 us
  matrix products  176 us (41%)
  waiting for transfers between devices  123 us (28%)
  local copies, waits for them, and re-layouts  79.7 us (18%)
  other arithmetic  31.7 us (7%)
  between operations  13.5 us (3%)
  starting transfers between devices  6.54 us (2%)
    dot_general x8, matrix products, tile_of(): jnp.einsum('tkgd,nkd->kgtn', queries, keys_now, preferred_element_type=jn...  62.4 us
    reduce_scatter x1, waiting for transfers between devices, per_device(): q_sum = lax.psum_scatter(q_part, 'text', scatter_dimension=0, tiled=True)  57.7 us
    unnamed x20, local copies, waits for them, and re-layouts  51.7 us
    dot_general x4, matrix products, backward(): jnp.einsum('kgtn,nkd->kgtd', score_grad, keys_now, preferred_element_type...  51.7 us
    all_gather x1, waiting for transfers between devices, per_device(): lax.all_gather(query_grad, 'text', axis=0, tiled=True)  46.9 us
    dot_general x4, matrix products, forward(): jnp.einsum('kgtn,nkd->kgtd', weights.astype(jnp.bfloat16), values_now, pr...  29.9 us
    reduce_sum x4, other arithmetic, forward(): total = total * fade + jnp.sum(weights, axis=-1)  29.2 us
    all_to_all x1, waiting for transfers between devices, per_device(): lax.all_to_all(text_states, 'text', split_axis=1, concat_axis=0, tiled=True)  18.3 us
  transfers between devices with their start and end apart: 3, of which 3 were waited for; matrix products, arithmetic and copies ran while one was open for 11% of the time, Pallas kernels for 0%

commit v1 on v0

--- a/solution.py
+++ b/solution.py
@@ -114,7 +114,10 @@
     weight_q = (column_steps[None, :] * (grid_levels.astype(jnp.float32) + soft)).astype(
         jnp.bfloat16
     )
-    spread = lax.all_to_all(text_states, "text", split_axis=1, concat_axis=0, tiled=True)
+    size = lax.axis_size("text")
+    pieces = jnp.stack(jnp.split(text_states, size, axis=1), axis=0)
+    pieces = lax.all_to_all(pieces, "text", split_axis=0, concat_axis=0)
+    spread = jnp.concatenate(pieces, axis=0)
     q_part = jnp.dot(spread, weight_q, preferred_element_type=jnp.float32)
     q_sum = lax.psum_scatter(q_part, "text", scatter_dimension=0, tiled=True)
     queries = q_sum.astype(jnp.bfloat16)

time: 433 us -> 412 us (0.952)
  blocking collectives: 0 us -> 54.3 us
  local copies, waits for them, and re-layouts: 79.7 us -> 28.3 us
  waiting for transfers between devices: 123 us -> 105 us
  starting transfers between devices: 6.54 us -> 0.22 us
    all_to_all x0 -> x1, blocking collectives: none -> 54.3 us  [per_device(): pieces = lax.all_to_all(pieces, 'text', split_axis=0, concat_axis=0)]
    unnamed x20 -> x18, local copies, waits for them, and re-layouts: 51.7 us -> 19 us
    all_to_all x1 -> x0, waiting for transfers between devices: 18.3 us -> none  [per_device(): lax.all_to_all(text_states, 'text', split_axis=1, concat_axis=0, tiled=True)]
    mul x1 -> x0, local copies, waits for them, and re-layouts: 17.6 us -> none  [per_device(): (weight_grad * column_steps[None, :] - 4.0 * centered * centered * center...]
    all_to_all x1 -> x0, starting transfers between devices: 6.32 us -> none  [per_device(): lax.all_to_all(text_states, 'text', split_axis=1, concat_axis=0, tiled=True)]
  transfers between devices with their start and end apart: 3 -> 2, of which waited for: 3 -> 2; matrix products, arithmetic and copies ran while one was open for 11% -> 4% of each run, Pallas kernels for 0% -> 0%
where the time goes in v1:
time: 412 us; the launch traced here: 411 us
  matrix products  177 us (43%)
  waiting for transfers between devices  105 us (25%)
  blocking collectives  54.3 us (13%)
  other arithmetic  32 us (8%)
  local copies, waits for them, and re-layouts  28.3 us (7%)
  between operations  13.6 us (3%)
    dot_general x8, matrix products, tile_of(): jnp.einsum('tkgd,nkd->kgtn', queries, keys_now, preferred_element_type=jn...  64.7 us
    reduce_scatter x1, waiting for transfers between devices, per_device(): q_sum = lax.psum_scatter(q_part, 'text', scatter_dimension=0, tiled=True)  58 us
    all_to_all x1, blocking collectives, per_device(): pieces = lax.all_to_all(pieces, 'text', split_axis=0, concat_axis=0)  54.3 us
    dot_general x4, matrix products, backward(): jnp.einsum('kgtn,nkd->kgtd', score_grad, keys_now, preferred_element_type...  51.9 us
    all_gather x1, waiting for transfers between devices, per_device(): lax.all_gather(query_grad, 'text', axis=0, tiled=True)  46.9 us
    dot_general x4, matrix products, forward(): jnp.einsum('kgtn,nkd->kgtd', weights.astype(jnp.bfloat16), values_now, pr...  29.9 us
    reduce_sum x4, other arithmetic, forward(): total = total * fade + jnp.sum(weights, axis=-1)  29.2 us
    unnamed x18, local copies, waits for them, and re-layouts  19 us
  transfers between devices with their start and end apart: 2, of which 2 were waited for; matrix products, arithmetic and copies ran while one was open for 4% of the time, Pallas kernels for 0%

profile of v1, /device:TPU:0, one launch (start us, length us, event | category | flops | bytes accessed | tf_op | source)
XLA Modules:
  0.0 411.3 jit_solution(1396605471433280631)
XLA Ops:
  8.5 54.3 %all_to_all.5 = bf16[4,128,2048]{2,1,0:T(8,128)(2,1)S(1)} all-to-all(bf16[4,128,2048]{2,1,0:T(8,128)(2,1)S(1)} %pad_maximum_fusion), channel_id=1, replica_groups=mesh['groups'=2,'text'=4,'image'=4] {'text'}, dimensions={0} | all-to-all | bytes 4194304 | tf_op jit(solution)/shard_map/all_to_all | solution.py:119
  64.1 13.3 %fusion.43 = f32[512,2048]{1,0:T(8,128)} fusion(bf16[512,2048]{1,0:T(8,128)(2,1)S(1)} %bitcast.140, bf16[2048,2048]{1,0:T(8,128)(2,1)} %param.14, f32[2048]{0:T(1024)} %param.16, f32[2048,2048]{1,0:T(8,128)} %param.15), kind=kOutput, calls=%fused_computation.50 | convolution fusion | flops 4332716032 | bytes 31465472 | tf_op jit(solution)/shard_map/dot_general | solution.py:121
  95.7 58.0 %reduce-scatter.2.cloned.1.call-done = f32[128,2048]{1,0:T(8,128)} async-done(((f32[512,2048]{1,0:T(8,128)}), f32[128,2048]{1,0:T(8,128)}) %reduce-scatter.2.cloned.1.call-update) | async-done | bytes 1048592 | tf_op jit(solution)/shard_map/reduce_scatter | solution.py:122
  155.3 95.8 %while.32 = (s32[]{:T(128)}, f32[2,8,128]{2,1,0:T(8,128)S(1)}, f32[2,8,128]{2,1,0:T(8,128)S(1)}, f32[2,8,128,128]{3,2,1,0:T(8,128)}, pred[128,4]{0,1:T(4,128)(4,...) while((s32[]{:T(128)}, f32[2,8,128]{2,1,0:T(8,128)S(1)}, ...), condition=%wide.region_8.9_spmd.clone, body=%wide.region_5.8_spmd.clone.sunk | while | flops 1712357376 | bytes 52192112 | solution.py:71
  155.3 8.1 %bitcast_reduce_fusion.2 = (f32[2,8,128]{2,1,0:T(8,128)S(1)}, f32[2,1601,128,8]{2,1,3,0:T(8,128)}) fusion(bf16[128,2,8,128]{3,0,2,1:T(8,128)(2,1)S(1)} %get-tuple-element.635, bf16[6404,2,128]{2,0,1:T(8,128)(2,1)} %get-tuple-element.634, s32[]{:T(128)S(6)} %select_n.117), kind=kOutput, calls=%fused_computation.1.clone.1 | convolution fusion | flops 845940736 | bytes 14471172 | tf_op jit(solution)/shard_map/while/body/eval_jaxpr/tkgd,nkd->kgtn/dot_general | solution.py:41
  170.8 7.5 %fusion.78 = f32[2,8,128,128]{3,2,1,0:T(8,128)S(1)} fusion(f32[2,1601,128,8]{2,1,3,0:T(8,128)} %get-tuple-element.592, f32[2,8,128]{2,1,0:T(8,128)S(1)} %maximum_select_fusion.2, pred[128]{0:T(512)(128)(4,1)S(1)} %dynamic-slice_bitcast_fusion.4, f32[2,8,128,128]{3,2,1,0:T(8,128)S(1)} %copy-done.2, bf16[6404,2,128]{2,0,1:T(8,128)(2,1)} %get-tuple-element.636, ...), kind=kOutput, calls=%fused_computation.8.clone.1 | convolution fusion | flops 853286912 | bytes 16109701 | tf_op jit(solution)/shard_map/while/body/eval_jaxpr/kgtn,nkd->kgtd/dot_general | solution.py:58
  179.2 8.1 %bitcast_reduce_fusion.2 = (f32[2,8,128]{2,1,0:T(8,128)S(1)}, f32[2,1601,128,8]{2,1,3,0:T(8,128)}) fusion(bf16[128,2,8,128]{3,0,2,1:T(8,128)(2,1)S(1)} %get-tuple-element.635, bf16[6404,2,128]{2,0,1:T(8,128)(2,1)} %get-tuple-element.634, s32[]{:T(128)S(6)} %select_n.117), kind=kOutput, calls=%fused_computation.1.clone.1 | convolution fusion | flops 845940736 | bytes 14471172 | tf_op jit(solution)/shard_map/while/body/eval_jaxpr/tkgd,nkd->kgtn/dot_general | solution.py:41
  187.3 7.3 %fusion.76 = f32[2,8,128]{2,1,0:T(8,128)S(1)} fusion(f32[2,1601,128,8]{2,1,3,0:T(8,128)} %get-tuple-element.592, f32[2,8,128]{2,1,0:T(8,128)S(1)} %maximum_select_fusion.2, pred[128]{0:T(512)(128)(4,1)S(1)} %dynamic-slice_bitcast_fusion.4), kind=kLoop, calls=%fused_computation.5.clone.1 | loop fusion | flops 13113344 | bytes 13131904 | tf_op jit(solution)/shard_map/while/body/eval_jaxpr/reduce_sum | solution.py:57
  194.7 7.5 %fusion.78 = f32[2,8,128,128]{3,2,1,0:T(8,128)S(1)} fusion(f32[2,1601,128,8]{2,1,3,0:T(8,128)} %get-tuple-element.592, f32[2,8,128]{2,1,0:T(8,128)S(1)} %maximum_select_fusion.2, pred[128]{0:T(512)(128)(4,1)S(1)} %dynamic-slice_bitcast_fusion.4, f32[2,8,128,128]{3,2,1,0:T(8,128)S(1)} %copy-done.2, bf16[6404,2,128]{2,0,1:T(8,128)(2,1)} %get-tuple-element.636, ...), kind=kOutput, calls=%fused_computation.8.clone.1 | convolution fusion | flops 853286912 | bytes 16109701 | tf_op jit(solution)/shard_map/while/body/eval_jaxpr/kgtn,nkd->kgtd/dot_general | solution.py:58
  203.2 8.1 %bitcast_reduce_fusion.2 = (f32[2,8,128]{2,1,0:T(8,128)S(1)}, f32[2,1601,128,8]{2,1,3,0:T(8,128)}) fusion(bf16[128,2,8,128]{3,0,2,1:T(8,128)(2,1)S(1)} %get-tuple-element.635, bf16[6404,2,128]{2,0,1:T(8,128)(2,1)} %get-tuple-element.634, s32[]{:T(128)S(6)} %select_n.117), kind=kOutput, calls=%fused_computation.1.clone.1 | convolution fusion | flops 845940736 | bytes 14471172 | tf_op jit(solution)/shard_map/while/body/eval_jaxpr/tkgd,nkd->kgtn/dot_general | solution.py:41
  218.6 7.5 %fusion.78 = f32[2,8,128,128]{3,2,1,0:T(8,128)S(1)} fusion(f32[2,1601,128,8]{2,1,3,0:T(8,128)} %get-tuple-element.592, f32[2,8,128]{2,1,0:T(8,128)S(1)} %maximum_select_fusion.2, pred[128]{0:T(512)(128)(4,1)S(1)} %dynamic-slice_bitcast_fusion.4, f32[2,8,128,128]{3,2,1,0:T(8,128)S(1)} %copy-done.2, bf16[6404,2,128]{2,0,1:T(8,128)(2,1)} %get-tuple-element.636, ...), kind=kOutput, calls=%fused_computation.8.clone.1 | convolution fusion | flops 853286912 | bytes 16109701 | tf_op jit(solution)/shard_map/while/body/eval_jaxpr/kgtn,nkd->kgtd/dot_general | solution.py:58
  227.1 8.1 %bitcast_reduce_fusion.2 = (f32[2,8,128]{2,1,0:T(8,128)S(1)}, f32[2,1601,128,8]{2,1,3,0:T(8,128)}) fusion(bf16[128,2,8,128]{3,0,2,1:T(8,128)(2,1)S(1)} %get-tuple-element.635, bf16[6404,2,128]{2,0,1:T(8,128)(2,1)} %get-tuple-element.634, s32[]{:T(128)S(6)} %select_n.117), kind=kOutput, calls=%fused_computation.1.clone.1 | convolution fusion | flops 845940736 | bytes 14471172 | tf_op jit(solution)/shard_map/while/body/eval_jaxpr/tkgd,nkd->kgtn/dot_general | solution.py:41
  242.6 7.5 %fusion.78 = f32[2,8,128,128]{3,2,1,0:T(8,128)S(1)} fusion(f32[2,1601,128,8]{2,1,3,0:T(8,128)} %get-tuple-element.592, f32[2,8,128]{2,1,0:T(8,128)S(1)} %maximum_select_fusion.2, pred[128]{0:T(512)(128)(4,1)S(1)} %dynamic-slice_bitcast_fusion.4, f32[2,8,128,128]{3,2,1,0:T(8,128)S(1)} %copy-done.2, bf16[6404,2,128]{2,0,1:T(8,128)(2,1)} %get-tuple-element.636, ...), kind=kOutput, calls=%fused_computation.8.clone.1 | convolution fusion | flops 853286912 | bytes 16109701 | tf_op jit(solution)/shard_map/while/body/eval_jaxpr/kgtn,nkd->kgtd/dot_general | solution.py:58
  253.3 84.5 %while.33 = (s32[]{:T(128)}, f32[2,8,128,128]{3,2,1,0:T(8,128)}, pred[128,4]{0,1:T(4,128)(4,1)S(1)}, bf16[6404,2,128]{2,0,1:T(8,128)(2,1)}, bf16[128,2,8,128]{3,...) while((s32[]{:T(128)}, f32[2,8,128,128]{3,2,1,0:T(8,128)}, ...), condition=%wide.region_11.12_spmd.clone, body=%wide.region_10.11_spmd.clone.sunk | while | flops 2544910336 | bytes 31930436 | solution.py:92
  253.5 8.2 %fusion.84 = f32[2,1601,128,8]{2,1,3,0:T(8,128)} fusion(bf16[128,2,8,128]{3,0,2,1:T(8,128)(2,1)S(1)} %get-tuple-element.673, bf16[6404,2,128]{2,0,1:T(8,128)(2,1)} %get-tuple-element.672, s32[]{:T(128)S(6)} %select_n.119), kind=kOutput, calls=%fused_computation.35.clone.1 | convolution fusion | flops 839385088 | bytes 14462980 | tf_op jit(solution)/shard_map/while/body/eval_jaxpr/tkgd,nkd->kgtn/dot_general | solution.py:41
  261.7 12.8 %fusion.85 = f32[2,8,128,128]{3,2,1,0:T(8,128)} fusion(f32[2,1601,128,8]{2,1,3,0:T(8,128)} %fusion.84, bf16[2,8,128,128]{3,2,1,0:T(8,128)(2,1)S(1)} %get-tuple-element.677, f32[2,8,128]{2,1,0:T(8,128)S(1)} %get-tuple-element.678, f32[2,8,128]{2,1,0:T(8,128)S(1)} %get-tuple-element.675, f32[2,8,128]{2,1,0:T(8,128)S(1)} %get-tuple-element.674, ...), kind=kOutput, calls=%fused_computation.32.clone.1 | convolution fusion | flops 1705525248 | bytes 17467008 | tf_op jit(solution)/shard_map/while/body/eval_jaxpr/kgtn,nkd->kgtd/dot_general | solution.py:88
  274.4 8.0 %fusion.84 = f32[2,1601,128,8]{2,1,3,0:T(8,128)} fusion(bf16[128,2,8,128]{3,0,2,1:T(8,128)(2,1)S(1)} %get-tuple-element.673, bf16[6404,2,128]{2,0,1:T(8,128)(2,1)} %get-tuple-element.672, s32[]{:T(128)S(6)} %select_n.119), kind=kOutput, calls=%fused_computation.35.clone.1 | convolution fusion | flops 839385088 | bytes 14462980 | tf_op jit(solution)/shard_map/while/body/eval_jaxpr/tkgd,nkd->kgtn/dot_general | solution.py:41
  282.5 13.1 %fusion.85 = f32[2,8,128,128]{3,2,1,0:T(8,128)} fusion(f32[2,1601,128,8]{2,1,3,0:T(8,128)} %fusion.84, bf16[2,8,128,128]{3,2,1,0:T(8,128)(2,1)S(1)} %get-tuple-element.677, f32[2,8,128]{2,1,0:T(8,128)S(1)} %get-tuple-element.678, f32[2,8,128]{2,1,0:T(8,128)S(1)} %get-tuple-element.675, f32[2,8,128]{2,1,0:T(8,128)S(1)} %get-tuple-element.674, ...), kind=kOutput, calls=%fused_computation.32.clone.1 | convolution fusion | flops 1705525248 | bytes 17467008 | tf_op jit(solution)/shard_map/while/body/eval_jaxpr/kgtn,nkd->kgtd/dot_general | solution.py:88
  295.5 8.0 %fusion.84 = f32[2,1601,128,8]{2,1,3,0:T(8,128)} fusion(bf16[128,2,8,128]{3,0,2,1:T(8,128)(2,1)S(1)} %get-tuple-element.673, bf16[6404,2,128]{2,0,1:T(8,128)(2,1)} %get-tuple-element.672, s32[]{:T(128)S(6)} %select_n.119), kind=kOutput, calls=%fused_computation.35.clone.1 | convolution fusion | flops 839385088 | bytes 14462980 | tf_op jit(solution)/shard_map/while/body/eval_jaxpr/tkgd,nkd->kgtn/dot_general | solution.py:41
  303.6 13.1 %fusion.85 = f32[2,8,128,128]{3,2,1,0:T(8,128)} fusion(f32[2,1601,128,8]{2,1,3,0:T(8,128)} %fusion.84, bf16[2,8,128,128]{3,2,1,0:T(8,128)(2,1)S(1)} %get-tuple-element.677, f32[2,8,128]{2,1,0:T(8,128)S(1)} %get-tuple-element.678, f32[2,8,128]{2,1,0:T(8,128)S(1)} %get-tuple-element.675, f32[2,8,128]{2,1,0:T(8,128)S(1)} %get-tuple-element.674, ...), kind=kOutput, calls=%fused_computation.32.clone.1 | convolution fusion | flops 1705525248 | bytes 17467008 | tf_op jit(solution)/shard_map/while/body/eval_jaxpr/kgtn,nkd->kgtd/dot_general | solution.py:88
  316.6 8.0 %fusion.84 = f32[2,1601,128,8]{2,1,3,0:T(8,128)} fusion(bf16[128,2,8,128]{3,0,2,1:T(8,128)(2,1)S(1)} %get-tuple-element.673, bf16[6404,2,128]{2,0,1:T(8,128)(2,1)} %get-tuple-element.672, s32[]{:T(128)S(6)} %select_n.119), kind=kOutput, calls=%fused_computation.35.clone.1 | convolution fusion | flops 839385088 | bytes 14462980 | tf_op jit(solution)/shard_map/while/body/eval_jaxpr/tkgd,nkd->kgtn/dot_general | solution.py:41
  324.7 13.1 %fusion.85 = f32[2,8,128,128]{3,2,1,0:T(8,128)} fusion(f32[2,1601,128,8]{2,1,3,0:T(8,128)} %fusion.84, bf16[2,8,128,128]{3,2,1,0:T(8,128)(2,1)S(1)} %get-tuple-element.677, f32[2,8,128]{2,1,0:T(8,128)S(1)} %get-tuple-element.678, f32[2,8,128]{2,1,0:T(8,128)S(1)} %get-tuple-element.675, f32[2,8,128]{2,1,0:T(8,128)S(1)} %get-tuple-element.674, ...), kind=kOutput, calls=%fused_computation.32.clone.1 | convolution fusion | flops 1705525248 | bytes 17467008 | tf_op jit(solution)/shard_map/while/body/eval_jaxpr/kgtn,nkd->kgtd/dot_general | solution.py:88
  340.0 46.9 %all-gather.2.cloned.1.call-done = bf16[512,2048]{0,1:T(8,128)(2,1)} async-done(((bf16[128,2048]{0,1:T(8,128)(2,1)}), bf16[512,2048]{0,1:T(8,128)(2,1)}) %all-gather.2.cloned.1.call-update) | async-done | bytes 2097168 | tf_op jit(solution)/shard_map/all_gather | solution.py:139
  386.9 17.6 %fusion.42 = f32[2048,2048]{1,0:T(8,128)} fusion(bf16[512,2048]{1,0:T(8,128)(2,1)S(1)} %bitcast.141, bf16[512,2048]{0,1:T(8,128)(2,1)} %all-gather.2.cloned.1.call-done, f32[2048]{0:T(1024)S(1)} %copy-done.5, f32[2048,2048]{1,0:T(8,128)} %param.15), kind=kOutput, calls=%fused_computation.47 | convolution fusion | flops 4357881856 | bytes 37756928 | tf_op jit(solution)/shard_map/dot_general | solution.py:137
  (79 shorter events, 53.3 us)
Async XLA Ops:
  6.5 147.1 %reduce-scatter.2.cloned.1.call-start = ((), (), s32[]{:S(2)}) async-start(), calls=%async_computation.2 | async-start | bytes 5242880 | tf_op jit(solution)/shard_map/reduce_scatter | solution.py:122
  62.8 1.4 copy-start
  64.1 13.6 %copy-start.6 = (s32[3]{0:T(128)S(1)}, s32[3]{0:T(128)}, u32[]{:S(2)}) copy-start(s32[3]{0:T(128)} %param.20) | copy-start | bytes 40
  77.5 309.4 %all-gather.2.cloned.1.call-start = ((), (), s32[]{:S(2)}) async-start(), calls=%async_computation.3 | async-start | bytes 2621440 | tf_op jit(solution)/shard_map/all_gather | solution.py:139
  78.0 17.4 %copy-start.4 = (s32[4]{0:T(128)S(1)}, s32[4]{0:T(128)}, u32[]{:S(2)}) copy-start(s32[4]{0:T(128)} %param.21) | copy-start | bytes 52
  155.3 15.5 %copy-start.2 = (f32[2,8,128,128]{3,2,1,0:T(8,128)S(1)}, f32[2,8,128,128]{3,2,1,0:T(8,128)}, u32[]{:S(2)}) copy-start(f32[2,8,128,128]{3,2,1,0:T(8,128)} %get-tuple-element.620) | copy-start | bytes 3145732 | tf_op jit(solution)/shard_map/while
  178.2 1.0 copy-start.3
  179.2 15.5 %copy-start.2 = (f32[2,8,128,128]{3,2,1,0:T(8,128)S(1)}, f32[2,8,128,128]{3,2,1,0:T(8,128)}, u32[]{:S(2)}) copy-start(f32[2,8,128,128]{3,2,1,0:T(8,128)} %get-tuple-element.620) | copy-start | bytes 3145732 | tf_op jit(solution)/shard_map/while
  202.2 1.0 copy-start.3
  203.2 15.5 %copy-start.2 = (f32[2,8,128,128]{3,2,1,0:T(8,128)S(1)}, f32[2,8,128,128]{3,2,1,0:T(8,128)}, u32[]{:S(2)}) copy-start(f32[2,8,128,128]{3,2,1,0:T(8,128)} %get-tuple-element.620) | copy-start | bytes 3145732 | tf_op jit(solution)/shard_map/while
  226.1 1.0 copy-start.3
  227.1 15.5 %copy-start.2 = (f32[2,8,128,128]{3,2,1,0:T(8,128)S(1)}, f32[2,8,128,128]{3,2,1,0:T(8,128)}, u32[]{:S(2)}) copy-start(f32[2,8,128,128]{3,2,1,0:T(8,128)} %get-tuple-element.620) | copy-start | bytes 3145732 | tf_op jit(solution)/shard_map/while
  250.0 1.0 copy-start.3
  253.2 133.6 %copy-start.1 = (bf16[4,128,2048]{2,1,0:T(8,128)(2,1)S(1)}, bf16[4,128,2048]{2,1,0:T(8,128)(2,1)}, u32[]{:S(2)}) copy-start(bf16[4,128,2048]{2,1,0:T(8,128)(2,1)} %copy-done) | copy-start | bytes 6291460
  253.3 133.6 %copy-start.5 = (f32[2048]{0:T(1024)S(1)}, f32[2048]{0:T(1024)}, u32[]{:S(2)}) copy-start(f32[2048]{0:T(1024)} %param.16) | copy-start | bytes 24580
Sparse Core Ops, SparseCore 0:
  77.6 75.9 reduce-scatter.1
  340.1 46.6 all-gather.1
